TPU v7x, 32 devices: a whole 2x2x4 slice. The times are simulated.
32 devices in a mesh: freq: 8 (over z, core), mode: 4 (over y, x).
Axes of the slice: x: 2, y: 2, z: 4, core: 2. Of those that a mesh axis runs over, the one named last changes fastest.
Arguments:
- sources: bfloat16 [16, 512, 2, 4096], P(None, None, None, ('freq', 'mode')), may hold values from -6 to 6
- mapping: bfloat16 [16, 2, 2048, 4096], P('freq', None, 'mode'), may hold values from -0.0625 to 0.0625
Outputs:
- pressure: bfloat16 [16, 512, 2, 2048], P(None, 'freq', None, 'mode')
All inputs are finite; a program needn't handle non-finite values.
Results may differ from a plain program's by a relative error of at most 0.0006.
Values may be sent and summed in bfloat16 or wider, within the bound.
A program may use at most 128 MiB of HBM per device.

v0:
```python
import jax
import jax.numpy as jnp
from jax import lax
from jax.sharding import PartitionSpec as P


def body(sources, mapping):
    freq_count = lax.axis_size("freq")
    mode_count = lax.axis_size("mode")
    bin_count = mapping.shape[0]
    slice_width = sources.shape[3]
    regrouped = lax.all_to_all(sources, "freq", split_axis=0, concat_axis=3, tiled=True)
    snapshots = regrouped.shape[1]
    blocked = regrouped.reshape(bin_count, snapshots, 2, 1, freq_count, slice_width)
    gathered = lax.all_gather(blocked, "mode", axis=3, tiled=True)
    complete = jnp.swapaxes(gathered, 3, 4).reshape(bin_count, snapshots, 2, -1)
    real_part = jnp.einsum(
        "bsm,bom->bso", complete[:, :, 0], mapping[:, 0], preferred_element_type=jnp.float32
    ) - jnp.einsum(
        "bsm,bom->bso", complete[:, :, 1], mapping[:, 1], preferred_element_type=jnp.float32
    )
    imag_part = jnp.einsum(
        "bsm,bom->bso", complete[:, :, 1], mapping[:, 0], preferred_element_type=jnp.float32
    ) + jnp.einsum(
        "bsm,bom->bso", complete[:, :, 0], mapping[:, 1], preferred_element_type=jnp.float32
    )
    field = jnp.stack([real_part, imag_part], axis=2)
    bins_total = bin_count * freq_count
    first_bin = lax.axis_index("freq") * bin_count
    bin_index = (first_bin + jnp.arange(bin_count, dtype=jnp.int32)).astype(jnp.float32)
    weights = ((bin_index + 1.0) / bins_total) ** 2
    local_energy = jnp.sum(weights[:, None, None, None] * field * field)
    energy = lax.psum(local_energy, ("freq", "mode"))
    energy = energy / (field.shape[1] * field.shape[3] * mode_count)
    factor = jnp.sqrt(bins_total / (energy + 1e-06))
    result = lax.all_to_all(
        (field * factor).astype(jnp.bfloat16), "freq", split_axis=1, concat_axis=0, tiled=True
    )
    return result


def solution(mesh):
    placed = (P(None, None, None, ("freq", "mode")), P("freq", None, "mode", None))
    return jax.shard_map(
        body, mesh=mesh, in_specs=placed, out_specs=P(None, "freq", None, "mode"), check_vma=False
    )
```

profile of v0, /device:TPU:0, one launch (start us, length us, event | category | flops | bytes accessed | tf_op | source)
XLA Modules:
  0.0 473.3 jit_solution(15611076914805232381)
XLA Ops:
  6.5 0.0 all-gather.3.cloned.1.call-start
  6.5 3.2 copy.16
  9.7 100.2 %all_to_all.33 = bf16[16,512,2,128]{3,1,2,0:T(8,128)(2,1)} all-to-all(bf16[16,512,2,128]{3,1,2,0:T(8,128)(2,1)S(1)} %copy.16), channel_id=1, replica_groups=mesh['freq'=8,'mode'=4] {'freq'}, dimensions={0} | all-to-all | bytes 8388608 | tf_op jit(solution)/shard_map/all_to_all | solution.py:12
  110.0 0.0 all-gather.3.cloned.1.call-update
  110.0 156.4 %all-gather.3.cloned.1.call-done = bf16[2,512,2,32,128]{4,1,2,0,3:T(8,128)(2,1)} async-done(((bf16[2,512,2,8,128]{4,1,2,0,3:T(8,128)(2,1)}), bf16[2,512,2,32,128]{4,1,2,0,3:T(8,128)(2,1)}) %all-gather.3.cloned.1.call-update) | async-done | bytes 16777232 | tf_op jit(solution)/shard_map/all_gather | solution.py:15
  266.4 22.3 %copy.18 = bf16[2,512,2,8,4,128]{5,4,3,1,0,2:T(4,128)(2,1)} copy(bf16[2,512,2,8,4,128]{5,1,2,0,3,4:T(8,128)(2,1)} %bitcast.46) | data formatting | bytes 33554432 | tf_op jit(solution)/shard_map/transpose | solution.py:16
  288.6 27.7 %reshape.16 = bf16[2,512,2,4096]{3,1,0,2:T(8,128)(2,1)} reshape(bf16[2,512,2,8,4,128]{5,4,3,1,0,2:T(4,128)(2,1)} %copy.18) | data formatting | bytes 33554432 | tf_op jit(solution)/shard_map/reshape | solution.py:16
  316.3 11.6 %fusion.2 = f32[2,512,512]{2,1,0:T(8,128)} fusion(bf16[2,512,2,4096]{3,1,0,2:T(8,128)(2,1)} %reshape.16, bf16[2,2,512,4096]{3,2,1,0:T(8,128)(2,1)} %param.3), kind=kOutput, calls=%fused_computation.4 | convolution fusion | flops 4294967296 | bytes 18874368 | tf_op jit(solution)/shard_map/bsm,bom->bso/dot_general | solution.py:19
  328.0 11.6 %fusion = f32[2,512,512]{2,1,0:T(8,128)} fusion(bf16[2,512,2,4096]{3,1,0,2:T(8,128)(2,1)} %reshape.16, bf16[2,2,512,4096]{3,2,1,0:T(8,128)(2,1)} %param.3), kind=kOutput, calls=%fused_computation.2 | convolution fusion | flops 4294967296 | bytes 18874368 | tf_op jit(solution)/shard_map/bsm,bom->bso/dot_general | solution.py:24
  339.6 10.9 %subtract_bitcast_fusion = f32[2,512,1,512]{3,1,0,2:T(8,128)S(1)} fusion(f32[2,512,512]{2,1,0:T(8,128)} %fusion.2, bf16[2,2,512,4096]{3,2,1,0:T(8,128)(2,1)} %param.3, bf16[2,512,2,4096]{3,1,0,2:T(8,128)(2,1)} %reshape.16), kind=kOutput, calls=%fused_computation.19 | convolution fusion | flops 4295491584 | bytes 20971520 | tf_op jit(solution)/shard_map/bsm,bom->bso/dot_general | solution.py:17
  350.4 12.4 %add_bitcast_fusion = f32[2,512,1,512]{3,1,0,2:T(8,128)} fusion(f32[2,512,512]{2,1,0:T(8,128)} %fusion, bf16[2,2,512,4096]{3,2,1,0:T(8,128)(2,1)} %param.3, bf16[2,512,2,4096]{3,1,0,2:T(8,128)(2,1)} %reshape.16), kind=kOutput, calls=%fused_computation.18 | convolution fusion | flops 4295491584 | bytes 20971520 | tf_op jit(solution)/shard_map/bsm,bom->bso/dot_general | solution.py:22
  362.9 3.4 fusion.12
  366.3 39.5 %psum.7 = f32[]{:T(128)} all-reduce(f32[]{:T(128)} %fusion.12), channel_id=1, replica_groups=mesh['freq'=8,'mode'=4] {'freq','mode'}, use_global_device_ids=true, to_apply=%region_1.0 | all-reduce | flops 1 | bytes 8 | tf_op jit(solution)/shard_map/psum | solution.py:33
  406.6 2.2 multiply_convert_fusion
  408.8 2.2 copy.21
  410.9 52.4 %all_to_all.34 = bf16[2,512,2,512]{3,0,2,1:T(2,128)(2,1)S(1)} all-to-all(bf16[2,512,2,512]{3,0,2,1:T(2,128)(2,1)S(1)} %copy.21), channel_id=1, replica_groups=mesh['freq'=8,'mode'=4] {'freq'}, dimensions={1} | all-to-all | bytes 4194304 | tf_op jit(solution)/shard_map/all_to_all | solution.py:36
  463.3 3.2 copy.22
  (1 shorter events, 0.0 us)
Async XLA Ops:
  6.5 259.8 %all-gather.3.cloned.1.call-start = ((), (), s32[]{:S(2)}) async-start(), calls=%async_computation.2 | async-start | bytes 20971520 | tf_op jit(solution)/shard_map/all_gather | solution.py:15
Sparse Core Ops, SparseCore 0:
  110.1 156.2 all-gather.2
where the time goes:
time: 474 us; the launch traced here: 473 us
  blocking collectives  192 us (41%)
  waiting for transfers between devices  156 us (33%)
  local copies, waits for them, and re-layouts  58.5 us (12%)
  matrix products  46.6 us (10%)
  between operations  14.2 us (3%)
  other arithmetic  5.6 us (1%)
    all_gather x1, waiting for transfers between devices, body(): gathered = lax.all_gather(blocked, 'mode', axis=3, tiled=True)  156 us
    all_to_all x1, blocking collectives, body(): lax.all_to_all(sources, 'freq', split_axis=0, concat_axis=3, tiled=True)  100 us
    all_to_all x1, blocking collectives, body(): lax.all_to_all((field * factor).astype(jnp.bfloat16), 'freq', split_axis=...  52.4 us
    psum x1, blocking collectives, body(): energy = lax.psum(local_energy, ('freq', 'mode'))  39.5 us
    reshape x1, local copies, waits for them, and re-layouts, body(): complete = jnp.swapaxes(gathered, 3, 4).reshape(bin_count, snapshots, 2, -1)  27.7 us
    transpose x1, local copies, waits for them, and re-layouts, body(): complete = jnp.swapaxes(gathered, 3, 4).reshape(bin_count, snapshots, 2, -1)  22.3 us
    dot_general x1, matrix products, body(): jnp.einsum('bsm,bom->bso', complete[:, :, 1], mapping[:, 0], preferred_el...  12.4 us
    dot_general x1, matrix products, body(): jnp.einsum('bsm,bom->bso', complete[:, :, 1], mapping[:, 1], preferred_el...  11.6 us
  transfers between devices with their start and end apart: 1, of which 1 were waited for; matrix products, arithmetic and copies ran while one was open for 0% of the time, Pallas kernels for 0%

commit v1 on v0

--- a/solution.py
+++ b/solution.py
@@ -12,7 +12,8 @@
     regrouped = lax.all_to_all(sources, "freq", split_axis=0, concat_axis=3, tiled=True)
     snapshots = regrouped.shape[1]
     blocked = regrouped.reshape(bin_count, snapshots, 2, 1, freq_count, slice_width)
-    gathered = lax.all_gather(blocked, "mode", axis=3, tiled=True)
+    state_next = lax.all_to_all(jnp.stack([blocked] * lax.axis_size("mode"), axis=0), "mode", 0, 0)
+    gathered = jnp.concatenate(state_next, axis=3)
     complete = jnp.swapaxes(gathered, 3, 4).reshape(bin_count, snapshots, 2, -1)
     real_part = jnp.einsum(
         "bsm,bom->bso", complete[:, :, 0], mapping[:, 0], preferred_element_type=jnp.float32

time: 474 us -> 516 us (1.089)
  waiting for transfers between devices: 156 us -> 182 us
  local copies, waits for them, and re-layouts: 58.5 us -> 81.9 us
  between operations: 14.2 us -> 0.82 us
  starting transfers between devices: 0.01 us -> 6.96 us
    all_to_all x0 -> x1, waiting for transfers between devices: none -> 182 us  [body(): lax.all_to_all(jnp.stack([blocked] * lax.axis_size('mode'), axis=0), 'mod...]
    all_gather x1 -> x0, waiting for transfers between devices: 156 us -> none  [body(): gathered = lax.all_gather(blocked, 'mode', axis=3, tiled=True)]
    transpose x1, local copies, waits for them, and re-layouts: 22.3 us -> 40.2 us  [body(): complete = jnp.swapaxes(gathered, 3, 4).reshape(bin_count, snapshots, 2, -1)]
    all_to_all x0 -> x1, starting transfers between devices: none -> 6.96 us  [body(): lax.all_to_all(jnp.stack([blocked] * lax.axis_size('mode'), axis=0), 'mod...]
    another operation x0 -> x1, local copies, waits for them, and re-layouts: none -> 5.98 us  [body(): jnp.stack([blocked] * lax.axis_size('mode'), axis=0)]
where the time goes in v1:
time: 516 us; the launch traced here: 515 us
  blocking collectives  191 us (37%)
  waiting for transfers between devices  182 us (35%)
  local copies, waits for them, and re-layouts  81.9 us (16%)
  matrix products  46.6 us (9%)
  starting transfers between devices  6.96 us (1%)
  other arithmetic  5.6 us (1%)
    all_to_all x1, waiting for transfers between devices, body(): lax.all_to_all(jnp.stack([blocked] * lax.axis_size('mode'), axis=0), 'mod...  182 us
    all_to_all x1, blocking collectives, body(): lax.all_to_all(sources, 'freq', split_axis=0, concat_axis=3, tiled=True)  100 us
    all_to_all x1, blocking collectives, body(): lax.all_to_all((field * factor).astype(jnp.bfloat16), 'freq', split_axis=...  52.9 us
    transpose x1, local copies, waits for them, and re-layouts, body(): complete = jnp.swapaxes(gathered, 3, 4).reshape(bin_count, snapshots, 2, -1)  40.2 us
    psum x1, blocking collectives, body(): energy = lax.psum(local_energy, ('freq', 'mode'))  37.5 us
    reshape x1, local copies, waits for them, and re-layouts, body(): complete = jnp.swapaxes(gathered, 3, 4).reshape(bin_count, snapshots, 2, -1)  27.7 us
    dot_general x1, matrix products, body(): jnp.einsum('bsm,bom->bso', complete[:, :, 1], mapping[:, 0], preferred_el...  12.4 us
    dot_general x1, matrix products, body(): jnp.einsum('bsm,bom->bso', complete[:, :, 1], mapping[:, 1], preferred_el...  11.6 us
  transfers between devices with their start and end apart: 1, of which 1 were waited for; matrix products, arithmetic and copies ran while one was open for 0% of the time, Pallas kernels for 0%

profile of v1, /device:TPU:0, one launch (start us, length us, event | category | flops | bytes accessed | tf_op | source)
XLA Modules:
  0.0 514.7 jit_solution(1200871743037257658)
XLA Ops:
  0.0 100.3 %all_to_all.38 = bf16[16,512,2,128]{3,2,1,0:T(2,128)(2,1)S(1)} all-to-all(bf16[16,512,2,128]{3,2,1,0:T(2,128)(2,1)} %param.2), channel_id=1, replica_groups=mesh['freq'=8,'mode'=4] {'freq'}, dimensions={0} | all-to-all | bytes 8388608 | tf_op jit(solution)/shard_map/all_to_all | solution.py:12
  100.3 2.7 copy.16
  103.0 6.0 %stack.12 = bf16[4,2,512,2,1,8,128]{6,5,2,1,3,4,0:T(8,128)(2,1)} broadcast(bf16[2,512,2,8,128]{4,3,1,0,2:T(8,128)(2,1)S(1)} %bitcast.49), dimensions={1,2,3,5,6} | broadcast | bytes 20971520 | tf_op jit(solution)/shard_map/stack | solution.py:15
  109.0 7.0 %all-to-all-start.1 = ((bf16[4,2,512,2,1,8,128]{6,5,2,1,3,4,0:T(8,128)(2,1)}), bf16[4,2,512,2,1,8,128]{6,5,2,1,3,4,0:T(8,128)(2,1)}, u32[]{:S(2)}, u32[]{:S(2)}) async-start(bf16[4,2,512,2,1,8,128]{6,5,2,1,3,4,0:T(8,128)(2,1)} %stack.12), calls=%async_computation.1 | async-start | bytes 33554432 | tf_op jit(solution)/shard_map/all_to_all | solution.py:15
  116.0 182.1 %all-to-all-done.1 = bf16[4,2,512,2,1,8,128]{6,5,2,1,3,4,0:T(8,128)(2,1)} async-done(((bf16[4,2,512,2,1,8,128]{6,5,2,1,3,4,0:T(8,128)(2,1)}), bf16[4,2,512,2,1,8,128]{6,5,2,1,3,4,0:T(8,128)(2,1)}, u32[]{:S(2)}, u32[]{:S(2)}) %all-to-all-start.1) | async-done | bytes 16777248 | tf_op jit(solution)/shard_map/all_to_all | solution.py:15
  298.1 40.2 %copy.8 = bf16[2,512,2,8,4,128]{5,4,3,1,0,2:T(4,128)(2,1)} copy(bf16[2,512,2,8,4,128]{5,3,1,0,2,4:T(8,128)(2,1)} %bitcast.4) | data formatting | bytes 33554432 | tf_op jit(solution)/shard_map/transpose | solution.py:17
  338.4 27.7 %reshape.22 = bf16[2,512,2,4096]{3,1,0,2:T(8,128)(2,1)} reshape(bf16[2,512,2,8,4,128]{5,4,3,1,0,2:T(4,128)(2,1)} %copy.8) | data formatting | bytes 33554432 | tf_op jit(solution)/shard_map/reshape | solution.py:17
  366.0 11.6 %fusion.2 = f32[2,512,512]{2,1,0:T(8,128)} fusion(bf16[2,512,2,4096]{3,1,0,2:T(8,128)(2,1)} %reshape.22, bf16[2,2,512,4096]{3,2,1,0:T(8,128)(2,1)} %param.3), kind=kOutput, calls=%fused_computation.4 | convolution fusion | flops 4294967296 | bytes 18874368 | tf_op jit(solution)/shard_map/bsm,bom->bso/dot_general | solution.py:20
  377.7 11.6 %fusion = f32[2,512,512]{2,1,0:T(8,128)} fusion(bf16[2,512,2,4096]{3,1,0,2:T(8,128)(2,1)} %reshape.22, bf16[2,2,512,4096]{3,2,1,0:T(8,128)(2,1)} %param.3), kind=kOutput, calls=%fused_computation.2 | convolution fusion | flops 4294967296 | bytes 18874368 | tf_op jit(solution)/shard_map/bsm,bom->bso/dot_general | solution.py:25
  389.3 10.9 %subtract_bitcast_fusion = f32[2,512,1,512]{3,1,0,2:T(8,128)S(1)} fusion(f32[2,512,512]{2,1,0:T(8,128)} %fusion.2, bf16[2,2,512,4096]{3,2,1,0:T(8,128)(2,1)} %param.3, bf16[2,512,2,4096]{3,1,0,2:T(8,128)(2,1)} %reshape.22), kind=kOutput, calls=%fused_computation.20 | convolution fusion | flops 4295491584 | bytes 20971520 | tf_op jit(solution)/shard_map/bsm,bom->bso/dot_general | solution.py:18
  400.2 12.4 %add_bitcast_fusion = f32[2,512,1,512]{3,1,0,2:T(8,128)} fusion(f32[2,512,512]{2,1,0:T(8,128)} %fusion, bf16[2,2,512,4096]{3,2,1,0:T(8,128)(2,1)} %param.3, bf16[2,512,2,4096]{3,1,0,2:T(8,128)(2,1)} %reshape.22), kind=kOutput, calls=%fused_computation.19 | convolution fusion | flops 4295491584 | bytes 20971520 | tf_op jit(solution)/shard_map/bsm,bom->bso/dot_general | solution.py:23
  412.6 3.4 fusion.12
  416.0 37.5 %psum.7 = f32[]{:T(128)} all-reduce(f32[]{:T(128)} %fusion.12), channel_id=1, replica_groups=mesh['freq'=8,'mode'=4] {'freq','mode'}, use_global_device_ids=true, to_apply=%region_1.0 | all-reduce | flops 1 | bytes 8 | tf_op jit(solution)/shard_map/psum | solution.py:34
  454.4 2.2 multiply_convert_fusion
  456.5 2.2 copy.11
  458.7 52.9 %all_to_all.39 = bf16[2,512,2,512]{3,0,2,1:T(2,128)(2,1)S(1)} all-to-all(bf16[2,512,2,512]{3,0,2,1:T(2,128)(2,1)S(1)} %copy.11), channel_id=1, replica_groups=mesh['freq'=8,'mode'=4] {'freq'}, dimensions={1} | all-to-all | bytes 4194304 | tf_op jit(solution)/shard_map/all_to_all | solution.py:37
  511.6 3.2 copy.12
  (1 shorter events, 0.0 us)
Async XLA Ops:
  109.0 189.1 %all-to-all-start.1 = ((bf16[4,2,512,2,1,8,128]{6,5,2,1,3,4,0:T(8,128)(2,1)}), bf16[4,2,512,2,1,8,128]{6,5,2,1,3,4,0:T(8,128)(2,1)}, u32[]{:S(2)}, u32[]{:S(2)}) async-start(bf16[4,2,512,2,1,8,128]{6,5,2,1,3,4,0:T(8,128)(2,1)} %stack.12), calls=%async_computation.1 | async-start | bytes 33554432 | tf_op jit(solution)/shard_map/all_to_all | solution.py:15
